TPU v7x, 32 devices: a whole 2x2x4 slice. The times are simulated.
32 devices in a mesh: dp: 8 (over z, y), row: 2 (over core), col: 2 (over x).
Axes of the slice: x: 2, y: 2, z: 4, core: 2. Of those that a mesh axis runs over, the one named last changes fastest.
Arguments:
- hidden_in: bfloat16 [4096, 960], P(('dp', 'col'), 'row')
- segment_ids: int32 [4096], P('dp'), may hold values from 0 to 4095, as said below
- position_ids: int32 [4096], P('dp'), may hold values from 0 to 2048, as said below
- attn_gain: float32 [960], P('row'), may hold values from 0.5 to 1.5
- query_weight: bfloat16 [960, 960], P('row', 'col')
- key_weight: bfloat16 [960, 320], P('row', 'col')
- value_matrix: bfloat16 [960, 320], P('row', 'col'), may hold values from -0.1875 to 0.1875
- output_weight: bfloat16 [960, 960], P('col', 'row'), may hold values from -0.75 to 0.75
- ffn_gain: float32 [960], P('row'), may hold values from 0.5 to 1.5
- gate_weight: bfloat16 [960, 2560], P('row', 'col'), may hold values from -0.1875 to 0.1875
- up_weight: bfloat16 [960, 2560], P('row', 'col'), may hold values from -0.1875 to 0.1875
- down_weight: bfloat16 [2560, 960], P('col', 'row'), may hold values from -0.125 to 0.125
- out_grad: bfloat16 [4096, 960], P(('dp', 'col'), 'row')
Outputs:
- hidden_out: bfloat16 [4096, 960], P(('dp', 'col'), 'row')
- hidden_in_grad: float32 [4096, 960], P(('dp', 'col'), 'row')
- attn_gain_grad: float32 [960], P('row')
- query_weight_grad: float32 [960, 960], P('row', 'col')
- key_weight_grad: float32 [960, 320], P('row', 'col')
- value_weight_grad: float32 [960, 320], P('row', 'col')
- output_weight_grad: float32 [960, 960], P('col', 'row')
- ffn_gain_grad: float32 [960], P('row')
- gate_weight_grad: float32 [2, 960, 1280], P('col', 'row', 'dp')
- up_weight_grad: float32 [2, 960, 1280], P('col', 'row', 'dp')
- down_weight_grad: float32 [2, 1280, 960], P('col', 'dp', 'row')
Inputs may be any that keep to these rules, and one draw needn't show every extreme that they name: `segment_ids`: segment numbers never fall from one token to the next, and the first token of each sequence of 512 tokens begins a new number. `position_ids`: within a document each token's position is one or two more than the previous token's; the first token of each sequence of 512 tokens has position 0.
All inputs are finite; a program needn't handle non-finite values.
Results may differ from a plain program's by a relative error of at most 0.02.
The roundings to bfloat16 on the way count: a program that leaves them out, or rounds other values in their place, can miss the bound.
Values may be sent and summed in bfloat16 or wider, within the bound.
A program may use at most 128 MiB of HBM per device.

v0:
```python
import jax
import jax.numpy as jnp
from jax import lax
from jax.sharding import PartitionSpec as P

MODEL_WIDTH = 960
QUERY_HEADS = 15
KEY_VALUE_HEADS = 5
HEAD_SIZE = 64
epsilon = 1e-05
rope_base = 10000.0
masked_score = -1e30


def rope_tables(position_row):
    half_size = HEAD_SIZE // 2
    frequency = rope_base ** (-(jnp.arange(half_size, dtype=jnp.float32) * 2.0) / HEAD_SIZE)
    angles = position_row.astype(jnp.float32)[:, None] * frequency[None, :]
    return (jnp.cos(angles), jnp.sin(angles))


def apply_rotary(values, cosine_table, sine_lookup, direction):
    half_size = values.shape[-1] // 2
    front_half = values[..., :half_size]
    back_half = values[..., half_size:]
    cosine_wide = cosine_table[:, None, :]
    sine_wide = direction * sine_lookup[:, None, :]
    return jnp.concatenate(
        [
            front_half * cosine_wide - back_half * sine_wide,
            back_half * cosine_wide + front_half * sine_wide,
        ],
        axis=-1,
    )


def matmul(left, right):
    return jnp.dot(left, right, preferred_element_type=jnp.float32)


def contract_rows(left, right):
    return lax.dot_general(
        left, right, (((0,), (0,)), ((), ())), preferred_element_type=jnp.float32
    )


def row_sums(values):
    return lax.psum(values, "row")


def gather_over_cols(values):
    return lax.all_gather(values, "col", axis=0, tiled=True)


def gather_over_rows(values):
    return lax.all_gather(values, "row", axis=0, tiled=True)


def sum_over_rows(partial_value):
    return lax.psum_scatter(partial_value, "row", scatter_dimension=0, tiled=True)


def sum_over_cols(partial_value):
    return lax.psum_scatter(partial_value, "col", scatter_dimension=0, tiled=True)


def to_heads(values):
    return lax.all_to_all(values, "col", split_axis=0, concat_axis=1, tiled=True)


def from_heads(values):
    return lax.all_to_all(values, "col", split_axis=1, concat_axis=0, tiled=True)


def norm_forward(residual, gain):
    mean_square = row_sums(jnp.sum(residual * residual, axis=1)) / MODEL_WIDTH
    inverse_rms = lax.rsqrt(mean_square + epsilon)
    unit_rows = residual * inverse_rms[:, None]
    return (unit_rows, inverse_rms, (unit_rows * gain[None, :]).astype(jnp.bfloat16))


def norm_backward(grad_normed, unit_rows, inverse_rms, gain):
    weighted = grad_normed * gain[None, :]
    inner_mean = row_sums(jnp.sum(weighted * unit_rows, axis=1)) / MODEL_WIDTH
    grad_input = inverse_rms[:, None] * (weighted - unit_rows * inner_mean[:, None])
    return (grad_input, jnp.sum(grad_normed * unit_rows, axis=0))


def attention_scores(query_group, key_group, allowed):
    scores = jnp.einsum(
        "qkgd,skd->kgqs", query_group, key_group, preferred_element_type=jnp.float32
    ) * HEAD_SIZE ** (-0.5)
    return jnp.where(allowed[None, None], scores, masked_score)


def on_device(
    hidden_in,
    segment_ids,
    position_ids,
    attn_gain,
    query_weight,
    key_weight,
    value_matrix,
    output_weight,
    ffn_gain,
    gate_weight,
    up_weight,
    down_weight,
    out_grad,
):
    n_rows = lax.axis_size("row")
    n_cols = lax.axis_size("col")
    sequence_length = segment_ids.shape[0]
    portion_length = sequence_length // (n_rows * n_cols)
    part_start = (lax.axis_index("row") * n_cols + lax.axis_index("col")) * portion_length
    query_cols = query_weight.shape[1]
    kv_cols = key_weight.shape[1]
    block_cols = query_cols + 2 * kv_cols
    heads_per_group = QUERY_HEADS // KEY_VALUE_HEADS
    ffn_cols = gate_weight.shape[1]
    residual = hidden_in.astype(jnp.float32)
    unit_one, inverse_one, normed_one = norm_forward(residual, attn_gain)
    normed_one_all = gather_over_cols(normed_one)
    proj_weight = jnp.concatenate([query_weight, key_weight, value_matrix], axis=1)
    projected = sum_over_rows(matmul(normed_one_all, proj_weight)).astype(jnp.bfloat16)
    grouped = to_heads(projected).reshape(portion_length, n_cols, block_cols)
    query_part = grouped[:, :, :query_cols].reshape(portion_length, n_cols * query_cols)
    key_portion = grouped[:, :, query_cols : query_cols + kv_cols].reshape(
        portion_length, n_cols * kv_cols
    )
    value_part = grouped[:, :, query_cols + kv_cols :].reshape(portion_length, n_cols * kv_cols)
    cosine_table, sine_lookup = rope_tables(
        lax.dynamic_slice_in_dim(position_ids, part_start, portion_length)
    )
    query_rotated = apply_rotary(
        query_part.astype(jnp.float32).reshape(portion_length, QUERY_HEADS, HEAD_SIZE),
        cosine_table,
        sine_lookup,
        1.0,
    ).astype(jnp.bfloat16)
    key_rotated = apply_rotary(
        key_portion.astype(jnp.float32).reshape(portion_length, KEY_VALUE_HEADS, HEAD_SIZE),
        cosine_table,
        sine_lookup,
        1.0,
    ).astype(jnp.bfloat16)
    key_token_rows, value_token_rows = (
        lax.all_gather(
            key_rotated.reshape(portion_length, KEY_VALUE_HEADS * HEAD_SIZE),
            ("row", "col"),
            axis=0,
            tiled=True,
        ),
        lax.all_gather(value_part, ("row", "col"), axis=0, tiled=True),
    )
    part_segments = lax.dynamic_slice_in_dim(segment_ids, part_start, portion_length)
    query_index = part_start + jnp.arange(portion_length, dtype=jnp.int32)
    key_index = jnp.arange(sequence_length, dtype=jnp.int32)
    allowed = (part_segments[:, None] == segment_ids[None, :]) & (
        key_index[None, :] <= query_index[:, None]
    )
    query_group = query_rotated.reshape(portion_length, KEY_VALUE_HEADS, heads_per_group, HEAD_SIZE)
    key_group = key_token_rows.reshape(sequence_length, KEY_VALUE_HEADS, HEAD_SIZE)
    value_group = value_token_rows.reshape(sequence_length, KEY_VALUE_HEADS, HEAD_SIZE)
    scores = attention_scores(query_group, key_group, allowed)
    row_max = jnp.max(scores, axis=-1, keepdims=True)
    log_total = row_max + jnp.log(jnp.sum(jnp.exp(scores - row_max), axis=-1, keepdims=True))
    attn_probs = jnp.exp(scores - log_total).astype(jnp.bfloat16)
    attended_output = (
        jnp.einsum("kgqs,skd->qkgd", attn_probs, value_group, preferred_element_type=jnp.float32)
        .astype(jnp.bfloat16)
        .reshape(portion_length, QUERY_HEADS * HEAD_SIZE)
    )
    attended_rows = from_heads(attended_output)
    attended_all = gather_over_rows(attended_rows)
    mid = residual + sum_over_cols(matmul(attended_all, output_weight))
    unit_two, inverse_two, normed_two = norm_forward(mid, ffn_gain)
    normed_two_all = gather_over_cols(normed_two)
    ffn_weight = jnp.concatenate([gate_weight, up_weight], axis=1)
    ffn_pre = sum_over_rows(matmul(normed_two_all, ffn_weight))
    gate_pre = ffn_pre[:, :ffn_cols]
    up_pre = ffn_pre[:, ffn_cols:]
    gate_sigmoid = jax.nn.sigmoid(gate_pre)
    gate_silu = gate_pre * gate_sigmoid
    inner_act = (gate_silu * up_pre).astype(jnp.bfloat16)
    inner_all = gather_over_rows(inner_act)
    final = mid + sum_over_cols(matmul(inner_all, down_weight))
    hidden_out = final.astype(jnp.bfloat16)
    grad_all = gather_over_cols(out_grad)
    inner_back = gather_over_rows(inner_act)
    down_wgrad = contract_rows(inner_back, grad_all)
    inner_grad = sum_over_rows(matmul(grad_all, down_weight.T))
    silu_slope = gate_sigmoid * (1.0 + gate_pre * (1.0 - gate_sigmoid))
    both_grad = jnp.concatenate(
        [
            (inner_grad * up_pre * silu_slope).astype(jnp.bfloat16),
            (inner_grad * gate_silu).astype(jnp.bfloat16),
        ],
        axis=1,
    )
    both_all = gather_over_rows(both_grad)
    normed_two_back = gather_over_cols(normed_two)
    ffn_wgrad = contract_rows(normed_two_back, both_all)
    normed_two_grad = sum_over_cols(matmul(both_all, ffn_weight.T))
    mid_part, ffn_gain_part = norm_backward(normed_two_grad, unit_two, inverse_two, ffn_gain)
    mid_grad = out_grad.astype(jnp.float32) + mid_part
    mid_grad_all = gather_over_cols(mid_grad.astype(jnp.bfloat16))
    attended_back = gather_over_rows(attended_rows)
    out_wgrad = contract_rows(attended_back, mid_grad_all)
    attended_gradient = to_heads(
        sum_over_rows(matmul(mid_grad_all, output_weight.T)).astype(jnp.bfloat16)
    )
    gradient_group = attended_gradient.reshape(
        portion_length, KEY_VALUE_HEADS, heads_per_group, HEAD_SIZE
    )
    attended_group = attended_output.reshape(
        portion_length, KEY_VALUE_HEADS, heads_per_group, HEAD_SIZE
    )
    grad_dot = jnp.transpose(
        jnp.sum(gradient_group.astype(jnp.float32) * attended_group.astype(jnp.float32), axis=-1),
        (1, 2, 0),
    )
    scores_again = attention_scores(query_group, key_group, allowed)
    prob_exact = jnp.exp(scores_again - log_total)
    value_gradient = jnp.einsum(
        "kgqs,qkgd->skd",
        prob_exact.astype(jnp.bfloat16),
        gradient_group,
        preferred_element_type=jnp.float32,
    )
    prob_grad = jnp.einsum(
        "qkgd,skd->kgqs", gradient_group, value_group, preferred_element_type=jnp.float32
    )
    score_grad = (prob_exact * (prob_grad - grad_dot[..., None]) * HEAD_SIZE ** (-0.5)).astype(
        jnp.bfloat16
    )
    query_grad = jnp.einsum(
        "kgqs,skd->qkgd", score_grad, key_group, preferred_element_type=jnp.float32
    )
    key_gradient = jnp.einsum(
        "kgqs,qkgd->skd", score_grad, query_group, preferred_element_type=jnp.float32
    )
    key_gradient_total, value_total = (
        lax.psum_scatter(
            key_gradient.reshape(sequence_length, KEY_VALUE_HEADS * HEAD_SIZE),
            ("row", "col"),
            scatter_dimension=0,
            tiled=True,
        ),
        lax.psum_scatter(
            value_gradient.reshape(sequence_length, KEY_VALUE_HEADS * HEAD_SIZE),
            ("row", "col"),
            scatter_dimension=0,
            tiled=True,
        ),
    )
    query_back = apply_rotary(
        query_grad.reshape(portion_length, QUERY_HEADS, HEAD_SIZE), cosine_table, sine_lookup, -1.0
    ).astype(jnp.bfloat16)
    key_backward = apply_rotary(
        key_gradient_total.reshape(portion_length, KEY_VALUE_HEADS, HEAD_SIZE),
        cosine_table,
        sine_lookup,
        -1.0,
    ).astype(jnp.bfloat16)
    regrouped = jnp.concatenate(
        [
            query_back.reshape(portion_length, n_cols, query_cols),
            key_backward.reshape(portion_length, n_cols, kv_cols),
            value_total.astype(jnp.bfloat16).reshape(portion_length, n_cols, kv_cols),
        ],
        axis=2,
    ).reshape(portion_length, n_cols * block_cols)
    proj_grad = from_heads(regrouped)
    proj_all = gather_over_rows(proj_grad)
    normed_one_back = gather_over_cols(normed_one)
    proj_wgrad = contract_rows(normed_one_back, proj_all)
    normed_one_grad = sum_over_cols(matmul(proj_all, proj_weight.T))
    in_part, attn_gain_part = norm_backward(normed_one_grad, unit_one, inverse_one, attn_gain)
    hidden_in_grad = mid_grad + in_part
    query_wgrad = proj_wgrad[:, :query_cols]
    key_wgrad = proj_wgrad[:, query_cols : query_cols + kv_cols]
    value_wgrad = proj_wgrad[:, query_cols + kv_cols :]
    col_gains = lax.psum((attn_gain_part, ffn_gain_part), "col")
    joined = lax.psum(
        (query_wgrad, key_wgrad, value_wgrad, out_wgrad, col_gains[0], col_gains[1]), "dp"
    )
    attn_totals = (joined[0], joined[1], joined[2], joined[3])
    gain_totals = (joined[4], joined[5])
    mlp_totals = (
        lax.psum_scatter(ffn_wgrad[None, :, :ffn_cols], "dp", scatter_dimension=2, tiled=True),
        lax.psum_scatter(ffn_wgrad[None, :, ffn_cols:], "dp", scatter_dimension=2, tiled=True),
        lax.psum_scatter(down_wgrad[None], "dp", scatter_dimension=1, tiled=True),
    )
    return (
        hidden_out,
        hidden_in_grad,
        gain_totals[0],
        attn_totals[0],
        attn_totals[1],
        attn_totals[2],
        attn_totals[3],
        gain_totals[1],
        mlp_totals[0],
        mlp_totals[1],
        mlp_totals[2],
    )


def solution(mesh):
    return jax.shard_map(
        on_device,
        mesh=mesh,
        in_specs=(
            P(("dp", "col"), "row"),
            P("dp"),
            P("dp"),
            P("row"),
            P("row", "col"),
            P("row", "col"),
            P("row", "col"),
            P("col", "row"),
            P("row"),
            P("row", "col"),
            P("row", "col"),
            P("col", "row"),
            P(("dp", "col"), "row"),
        ),
        out_specs=(
            P(("dp", "col"), "row"),
            P(("dp", "col"), "row"),
            P("row"),
            P("row", "col"),
            P("row", "col"),
            P("row", "col"),
            P("col", "row"),
            P("row"),
            P("col", "row", "dp"),
            P("col", "row", "dp"),
            P("col", "dp", "row"),
        ),
        check_vma=False,
    )
```

profile of v0, /device:TPU:0, one launch (start us, length us, event | category | flops | bytes accessed | tf_op | source)
XLA Modules:
  0.0 676.4 jit_solution(15995002472358062000)
XLA Ops:
  8.4 2.6 psum.84
  12.1 9.8 %all_gather.34 = bf16[512,480]{0,1:T(8,128)(2,1)S(1)} all-gather(bf16[256,480]{0,1:T(8,128)(2,1)S(1)} %fusion.10), channel_id=1, replica_groups=mesh['dp'=8,'row'=2,'col'=2] {'col'}, dimensions={0}, use_global_device_ids=true | all-gather | bytes 737280 | tf_op jit(solution)/shard_map/all_gather | solution.py:52
  24.2 3.2 fusion.18
  28.5 9.7 %reduce-scatter.11.cloned.1.call-done = f32[256,800]{0,1:T(8,128)} async-done(((f32[512,800]{0,1:T(8,128)}), f32[256,800]{0,1:T(8,128)}) %reduce-scatter.11.cloned.1.call-update) | async-done | bytes 819216 | tf_op jit(solution)/shard_map/reduce_scatter | solution.py:60
  38.2 1.9 copy_bitcast_fusion.1
  40.2 3.5 all-to-all-start
  43.8 7.3 %all-to-all-done = bf16[2,128,800]{1,2,0:T(8,128)(2,1)S(1)} async-done(((bf16[2,128,800]{1,2,0:T(8,128)(2,1)}), bf16[2,128,800]{1,2,0:T(8,128)(2,1)S(1)}, u32[]{:S(2)}, u32[]{:S(2)}) %all-to-all-start) | async-done | bytes 409632 | tf_op jit(solution)/shard_map/all_to_all | solution.py:68
  51.2 10.6 %all_gather.35 = bf16[512,320]{0,1:T(8,128)(2,1)S(1)} all-gather(bf16[128,320]{0,1:T(8,128)(2,1)S(1)} %bitcast.147), channel_id=1, replica_groups=mesh['dp'=8,'row'=2,'col'=2] {'row','col'}, dimensions={0}, use_global_device_ids=true | all-gather | bytes 409600 | tf_op jit(solution)/shard_map/all_gather | solution.py:154
  61.8 10.6 %all_gather.36 = bf16[512,320]{0,1:T(8,128)(2,1)S(1)} all-gather(bf16[128,320]{0,1:T(8,128)(2,1)S(1)} %bitcast.148), channel_id=1, replica_groups=mesh['dp'=8,'row'=2,'col'=2] {'row','col'}, dimensions={0}, use_global_device_ids=true | all-gather | bytes 409600 | tf_op jit(solution)/shard_map/all_gather | solution.py:148
  75.3 8.1 %all_to_all.67 = bf16[128,2,480]{0,2,1:T(8,128)(2,1)S(1)} all-to-all(bf16[128,2,480]{0,2,1:T(8,128)(2,1)S(1)} %bitcast.135), channel_id=1, replica_groups=mesh['dp'=8,'row'=2,'col'=2] {'col'}, dimensions={1} | all-to-all | bytes 491520 | tf_op jit(solution)/shard_map/all_to_all | solution.py:72
  83.4 2.2 all_gather.37
  87.1 9.4 %all_gather.40 = bf16[512,480]{0,1:T(8,128)(2,1)S(1)} all-gather(bf16[256,480]{0,1:T(8,128)(2,1)S(1)} %copy-done.9), channel_id=1, replica_groups=mesh['dp'=8,'row'=2,'col'=2] {'col'}, dimensions={0}, use_global_device_ids=true | all-gather | bytes 737280 | tf_op jit(solution)/shard_map/all_gather | solution.py:52
  96.5 2.3 fusion.39
  98.9 2.5 constant_dynamic-update-slice_fusion.1
  101.4 2.5 constant_dynamic-update-slice_fusion
  103.9 3.6 reduce-scatter.13.cloned.1.call-done
  108.6 2.5 psum.85
  111.2 8.7 %all_gather.38 = bf16[512,480]{0,1:T(8,128)(2,1)S(1)} all-gather(bf16[256,480]{0,1:T(8,128)(2,1)S(1)} %multiply_convert_fusion.3), channel_id=1, replica_groups=mesh['dp'=8,'row'=2,'col'=2] {'col'}, dimensions={0}, use_global_device_ids=true | all-gather | bytes 737280 | tf_op jit(solution)/shard_map/all_gather | solution.py:52
  119.9 5.6 fusion.37
  125.6 13.3 %reduce-scatter.15.cloned.1.call-done = f32[256,2560]{1,0:T(8,128)} async-done(((f32[512,2560]{1,0:T(8,128)}), f32[256,2560]{1,0:T(8,128)}) %reduce-scatter.15.cloned.1.call-update) | async-done | bytes 2621456 | tf_op jit(solution)/shard_map/reduce_scatter | solution.py:60
  138.9 3.7 multiply_convert_fusion.1
  143.9 12.8 %all-gather.5.cloned.1.call-done = bf16[512,2560]{1,0:T(8,128)(2,1)} async-done(((bf16[256,2560]{1,0:T(8,128)(2,1)}), bf16[512,2560]{1,0:T(8,128)(2,1)}) %all-gather.5.cloned.1.call-update) | async-done | bytes 2621456 | tf_op jit(solution)/shard_map/all_gather | solution.py:56
  156.6 4.9 fusion.40
  161.6 21.0 %reduce-scatter.21.cloned.1.call-done = f32[256,480]{0,1:T(8,128)} async-done(((f32[512,480]{0,1:T(8,128)}), f32[256,480]{0,1:T(8,128)}) %reduce-scatter.21.cloned.1.call-update) | async-done | bytes 491536 | tf_op jit(solution)/shard_map/reduce_scatter | solution.py:64
  184.4 2.4 psum.86
  188.1 8.7 %all_gather.42 = bf16[512,480]{0,1:T(8,128)(2,1)S(1)} all-gather(bf16[256,480]{0,1:T(8,128)(2,1)S(1)} %fusion.33), channel_id=1, replica_groups=mesh['dp'=8,'row'=2,'col'=2] {'col'}, dimensions={0}, use_global_device_ids=true | all-gather | bytes 737280 | tf_op jit(solution)/shard_map/all_gather | solution.py:52
  198.2 8.4 %reduce-scatter.23.cloned.1.call-done = f32[256,480]{0,1:T(8,128)} async-done(((f32[512,480]{0,1:T(8,128)}), f32[256,480]{0,1:T(8,128)}) %reduce-scatter.23.cloned.1.call-update) | async-done | bytes 491536 | tf_op jit(solution)/shard_map/reduce_scatter | solution.py:60
  207.7 8.3 %all_to_all.68 = bf16[2,128,480]{1,2,0:T(8,128)(2,1)S(1)} all-to-all(bf16[2,128,480]{1,2,0:T(8,128)(2,1)S(1)} %copy_bitcast_fusion.3), channel_id=1, replica_groups=mesh['dp'=8,'row'=2,'col'=2] {'col'}, dimensions={0} | all-to-all | bytes 491520 | tf_op jit(solution)/shard_map/all_to_all | solution.py:68
  216.0 4.1 fusion.22
  221.3 3.8 fusion.2
  228.7 2.1 fusion.41
  231.6 11.2 %reduce-scatter.27.cloned.1.call-done = f32[128,320]{0,1:T(8,128)} async-done(((f32[512,320]{0,1:T(8,128)}), f32[128,320]{0,1:T(8,128)}) %reduce-scatter.27.cloned.1.call-update) | async-done | bytes 163856 | tf_op jit(solution)/shard_map/reduce_scatter | solution.py:250
  244.3 23.4 %reduce-scatter.25.cloned.1.call-done = f32[128,320]{0,1:T(8,128)} async-done(((f32[512,320]{0,1:T(8,128)}), f32[128,320]{0,1:T(8,128)}) %reduce-scatter.25.cloned.1.call-update) | async-done | bytes 163856 | tf_op jit(solution)/shard_map/reduce_scatter | solution.py:244
  269.9 9.2 %all_to_all.69 = bf16[128,2,800]{0,2,1:T(8,128)(2,1)S(1)} all-to-all(bf16[128,2,800]{0,2,1:T(8,128)(2,1)S(1)} %pad_maximum_fusion.2), channel_id=1, replica_groups=mesh['dp'=8,'row'=2,'col'=2] {'col'}, dimensions={1} | all-to-all | bytes 819200 | tf_op jit(solution)/shard_map/all_to_all | solution.py:72
  279.1 2.4 all_gather.43
  284.1 3.7 convolution_bitcast_fusion
  287.8 6.5 copy.78
  294.3 3.1 fusion.38
  297.5 3.2 fusion.44
  300.7 2.5 slice_bitcast_fusion
  303.2 6.4 copy.76
  309.7 6.5 copy.77
  323.4 4.9 all-reduce.5
  328.3 22.6 %all-reduce.3 = (f32[480]{0:T(512)}, f32[480]{0:T(512)}) all-reduce(f32[480]{0:T(512)S(1)} %get-tuple-element.68, f32[480]{0:T(512)S(1)} %get-tuple-element.69), channel_id=1, replica_groups=mesh['dp'=8,'row'=2,'col'=2] {'dp'}, use_global_device_ids=true, to_apply=%region_23.24 | all-reduce | flops 960 | bytes 7680 | tf_op jit(solution)/shard_map/psum | solution.py:285
  350.9 2.4 psum.87
  353.4 2.3 fusion.14
  355.7 304.2 %all-reduce.8.cloned.1.call-done = (f32[480,480]{0,1:T(8,128)}, f32[480,160]{0,1:T(8,128)}, f32[480,160]{0,1:T(8,128)}, f32[480,480]{1,0:T(8,128)}, f32[1,480,12...) async-done(((f32[480,480]{0,1:T(8,128)}, f32[480,160]{0,1:T(8,128)}, f32[480,160]{0,1:T(8,128)}, f32[480,480]{1,0:T(8,128)}, ...) | async-done | bytes 9830416 | tf_op jit(solution)/shard_map/psum | solution.py:285
  659.9 2.5 copy.79
  (160 shorter events, 44.3 us)
Async XLA Ops:
  7.2 89.3 %copy-start = (bf16[1280,480]{0,1:T(8,128)(2,1)S(1)}, bf16[1280,480]{0,1:T(8,128)(2,1)}, u32[]{:S(2)}) copy-start(bf16[1280,480]{0,1:T(8,128)(2,1)} %param.24) | copy-start | bytes 3686404
  7.2 31.0 %reduce-scatter.11.cloned.1.call-start = ((), (), s32[]{:S(2)}) async-start(), calls=%async_computation.14 | async-start | bytes 2457600 | tf_op jit(solution)/shard_map/reduce_scatter | solution.py:60
  21.8 5.7 copy-start.11
  23.1 4.4 copy-start.25
  24.2 3.3 copy-start.27
  24.2 3.3 copy-start.33
  40.2 11.0 %all-to-all-start = ((bf16[2,128,800]{1,2,0:T(8,128)(2,1)}), bf16[2,128,800]{1,2,0:T(8,128)(2,1)S(1)}, u32[]{:S(2)}, u32[]{:S(2)}) async-start(bf16[2,128,800]{1,2,0:T(8,128)(2,1)} %copy_bitcast_fusion.1), calls=%async_computation.1 | async-start | bytes 819200 | tf_op jit(solution)/shard_map/all_to_all | solution.py:68
  43.6 63.8 %reduce-scatter.13.cloned.1.call-start = ((), (), s32[]{:S(2)}) async-start(), calls=%async_computation.15 | async-start | bytes 1474560 | tf_op jit(solution)/shard_map/reduce_scatter | solution.py:64
  61.8 12.4 %copy-start.22 = (bf16[512,320]{0,1:T(8,128)(2,1)}, bf16[512,320]{0,1:T(8,128)(2,1)S(1)}, u32[]{:S(2)}) copy-start(bf16[512,320]{0,1:T(8,128)(2,1)S(1)} %all_gather.35) | copy-start | bytes 983044
  72.4 0.9 copy-start.8
  72.6 1.6 copy-start.15
  73.3 1.9 copy-start.1
  74.2 1.1 copy-start.31
  74.2 11.4 %copy-start.13 = (bf16[480,480]{1,0:T(8,128)(2,1)S(1)}, bf16[480,480]{1,0:T(8,128)(2,1)}, u32[]{:S(2)}) copy-start(bf16[480,480]{1,0:T(8,128)(2,1)} %param.20) | copy-start | bytes 1382404
  75.3 8.1 %copy-start.20 = (bf16[5,64,3,128]{3,1,2,0:T(8,128)(2,1)}, bf16[5,64,3,128]{3,1,2,0:T(8,128)(2,1)S(1)}, u32[]{:S(2)}) copy-start(bf16[5,64,3,128]{3,1,2,0:T(8,128)(2,1)S(1)} %convolution_convert_fusion) | copy-start | bytes 737284
  75.3 11.7 %copy-start.9 = (bf16[256,480]{0,1:T(8,128)(2,1)S(1)}, bf16[256,480]{0,1:T(8,128)(2,1)}, u32[]{:S(2)}) copy-start(bf16[256,480]{0,1:T(8,128)(2,1)} %param.25) | copy-start | bytes 737284
  87.0 38.6 %reduce-scatter.19.cloned.1.call-start = ((), (), s32[]{:S(2)}) async-start(), calls=%async_computation.19 | async-start | bytes 3932160 | tf_op jit(solution)/shard_map/reduce_scatter | solution.py:60
  96.5 2.3 copy-start.7
  98.9 8.6 %copy-start.3 = (bf16[256,480]{0,1:T(8,128)(2,1)S(1)}, bf16[256,480]{0,1:T(8,128)(2,1)}, u32[]{:S(2)}) copy-start(bf16[256,480]{0,1:T(8,128)(2,1)} %param.13) | copy-start | bytes 737284
  98.9 40.1 %reduce-scatter.15.cloned.1.call-start = ((), (), s32[]{:S(2)}) async-start(), calls=%async_computation.16 | async-start | bytes 7864320 | tf_op jit(solution)/shard_map/reduce_scatter | solution.py:60
  101.4 9.6 %copy-start.29 = (f32[480]{0:T(512)S(1)}, f32[480]{0:T(512)}, u32[]{:S(2)}) copy-start(f32[480]{0:T(512)} %param.21) | copy-start | bytes 5764
  125.5 31.1 %all-gather.5.cloned.1.call-start = ((), (), s32[]{:S(2)}) async-start(), calls=%async_computation.20 | async-start | bytes 3932160 | tf_op jit(solution)/shard_map/all_gather | solution.py:56
  143.8 38.7 %reduce-scatter.21.cloned.1.call-start = ((), (), s32[]{:S(2)}) async-start(), calls=%async_computation.21 | async-start | bytes 1474560 | tf_op jit(solution)/shard_map/reduce_scatter | solution.py:64
  161.5 45.1 %reduce-scatter.23.cloned.1.call-start = ((), (), s32[]{:S(2)}) async-start(), calls=%async_computation.22 | async-start | bytes 1474560 | tf_op jit(solution)/shard_map/reduce_scatter | solution.py:60
  186.8 10.0 %copy-start.14 = (bf16[480,480]{1,0:T(8,128)(2,1)S(1)}, bf16[480,480]{1,0:T(8,128)(2,1)}, u32[]{:S(2)}) copy-start(bf16[480,480]{1,0:T(8,128)(2,1)} %param.20) | copy-start | bytes 1382404
  198.2 44.6 %reduce-scatter.27.cloned.1.call-start = ((), (), s32[]{:S(2)}) async-start(), calls=%async_computation.24 | async-start | bytes 819200 | tf_op jit(solution)/shard_map/reduce_scatter | solution.py:250
  216.0 4.1 copy-start.21
  220.1 47.7 %reduce-scatter.25.cloned.1.call-start = ((), (), s32[]{:S(2)}) async-start(), calls=%async_computation.23 | async-start | bytes 819200 | tf_op jit(solution)/shard_map/reduce_scatter | solution.py:244
  221.3 5.1 copy-start.16
  221.3 5.1 copy-start.18
  225.1 1.3 copy-start.2
  228.1 56.1 %all-gather.3.cloned.1.call-start = ((), (), s32[]{:S(2)}) async-start(), calls=%async_computation.17 | async-start | bytes 1966080 | tf_op jit(solution)/shard_map/all_gather | solution.py:56
  228.6 93.4 %reduce-scatter.29.cloned.1.call-start = ((), (), s32[]{:S(2)}) async-start(), calls=%async_computation.25 | async-start | bytes 1474560 | tf_op jit(solution)/shard_map/reduce_scatter | solution.py:64
  267.8 14.6 %copy-start.26 = (bf16[480,160]{1,0:T(8,128)(2,1)S(1)}, bf16[480,160]{1,0:T(8,128)(2,1)}, u32[]{:S(2)}) copy-start(bf16[480,160]{1,0:T(8,128)(2,1)} %copy-done.25) | copy-start | bytes 460804
  267.8 14.6 %copy-start.28 = (bf16[480,160]{1,0:T(8,128)(2,1)S(1)}, bf16[480,160]{1,0:T(8,128)(2,1)}, u32[]{:S(2)}) copy-start(bf16[480,160]{1,0:T(8,128)(2,1)} %copy-done.27) | copy-start | bytes 460804
  267.8 14.6 %copy-start.34 = (bf16[480,480]{1,0:T(8,128)(2,1)S(1)}, bf16[480,480]{1,0:T(8,128)(2,1)}, u32[]{:S(2)}) copy-start(bf16[480,480]{1,0:T(8,128)(2,1)} %param.17) | copy-start | bytes 1382404
  281.5 0.9 copy-start.5
  284.1 69.3 %reduce-scatter.17.cloned.1.call-start = ((), (), s32[]{:S(2)}) async-start(), calls=%async_computation.18 | async-start | bytes 1474560 | tf_op jit(solution)/shard_map/reduce_scatter | solution.py:64
  297.4 362.4 %all-reduce.8.cloned.1.call-start = ((), (), s32[]{:S(2)}) async-start(), calls=%async_computation.26 | async-start | bytes 20971520 | tf_op jit(solution)/shard_map/psum | solution.py:285
  309.7 7.9 %copy-start.12 = (bf16[512,480]{0,1:T(8,128)(2,1)S(1)}, bf16[512,480]{0,1:T(8,128)(2,1)}, u32[]{:S(2)}) copy-start(bf16[512,480]{0,1:T(8,128)(2,1)} %copy-done.11) | copy-start | bytes 1474564
  316.2 1.4 copy-start.6
  320.2 1.9 copy-start.30
  320.2 3.2 copy-start.32
  320.2 33.2 %copy-start.4 = (f32[256,480]{0,1:T(8,128)S(1)}, f32[256,480]{0,1:T(8,128)}, u32[]{:S(2)}) copy-start(f32[256,480]{0,1:T(8,128)} %reduce-scatter.21.cloned.1.call-done) | copy-start | bytes 1474564
  320.2 33.2 %copy-start.10 = (bf16[256,480]{0,1:T(8,128)(2,1)S(1)}, bf16[256,480]{0,1:T(8,128)(2,1)}, u32[]{:S(2)}) copy-start(bf16[256,480]{0,1:T(8,128)(2,1)} %param.25) | copy-start | bytes 737284
  662.3 5.1 copy-start.24
  662.4 5.8 copy-start.23
  662.4 6.5 copy-start.19
  (2 other events, 1.5 us)
Sparse Core Ops, SparseCore 0:
  27.6 10.5 reduce-scatter.10
  87.1 20.2 reduce-scatter.12
  109.7 10.6 reduce-scatter.18
  125.6 13.2 reduce-scatter.14
  143.9 12.6 all-gather.4
  161.7 20.8 reduce-scatter.20
  198.3 8.3 reduce-scatter.22
  220.2 22.5 reduce-scatter.26
  245.3 22.4 reduce-scatter.24
  269.7 9.4 all-gather.2
  284.2 19.6 reduce-scatter.28
  306.6 19.6 reduce-scatter.16
  332.3 327.4 all-reduce.7
where the time goes:
time: 678 us; the launch traced here: 676 us
  waiting for transfers between devices  416 us (61%)
  blocking collectives  125 us (18%)
  matrix products  45.8 us (7%)
  local copies, waits for them, and re-layouts  44.9 us (7%)
  other arithmetic  25.6 us (4%)
  between operations  15.1 us (2%)
    psum x1, waiting for transfers between devices, on_device(): lax.psum((query_wgrad, key_wgrad, value_wgrad, out_wgrad, col_gains[0], c...  304 us
    all_gather x4, blocking collectives, gather_over_cols(): return lax.all_gather(values, 'col', axis=0, tiled=True)  36.6 us
    reduce_scatter x4, waiting for transfers between devices, sum_over_rows(): lax.psum_scatter(partial_value, 'row', scatter_dimension=0, tiled=True)  31.5 us
    reduce_scatter x4, waiting for transfers between devices, sum_over_cols(): lax.psum_scatter(partial_value, 'col', scatter_dimension=0, tiled=True)  24.5 us
    dot_general x8, matrix products, matmul(): return jnp.dot(left, right, preferred_element_type=jnp.float32)  23.5 us
    reduce_scatter x1, waiting for transfers between devices, on_device(): lax.psum_scatter(key_gradient.reshape(sequence_length, KEY_VALUE_HEADS *...  23.4 us
    psum x1, blocking collectives, on_device(): lax.psum((query_wgrad, key_wgrad, value_wgrad, out_wgrad, col_gains[0], c...  22.6 us
    unnamed x85, local copies, waits for them, and re-layouts  18.3 us
  transfers between devices with their start and end apart: 14, of which 10 were waited for; matrix products, arithmetic and copies ran while one was open for 10% of the time, Pallas kernels for 0%

commit v1 on v0

--- a/solution.py
+++ b/solution.py
@@ -10,6 +10,33 @@
 epsilon = 1e-05
 rope_base = 10000.0
 masked_score = -1e30
+
+
+def threads_remake(here_x, array_dim):
+    v_now = list(here_x.shape[1:])
+    v_now[array_dim] *= here_x.shape[0]
+    work_now = jnp.moveaxis(here_x, 0, array_dim).reshape(v_now)
+    return work_now
+
+
+def do_entries(view, mesh_ax):
+    row_out = lax.axis_size(mesh_ax)
+    carry_in, y2 = (row_out, lax.axis_index(mesh_ax))
+    earlier, w2 = (view[None], 1)
+    while w2 < carry_in:
+        u_next = list(map(lambda d: (d, d ^ w2), range(carry_in)))
+        side_arr = lax.ppermute(earlier, axis_name=mesh_ax, perm=u_next)
+        o_now = y2 & w2 == 0
+        earlier = jnp.concatenate(
+            [jnp.where(o_now, earlier, side_arr), jnp.where(o_now, side_arr, earlier)]
+        )
+        w2 *= 2
+    return earlier
+
+
+def plan_limits(chunk, x0, on_dim):
+    r2 = threads_remake(do_entries(chunk, x0), on_dim)
+    return r2
 
 
 def rope_tables(position_row):
@@ -49,7 +76,7 @@
 
 
 def gather_over_cols(values):
-    return lax.all_gather(values, "col", axis=0, tiled=True)
+    return plan_limits(values, "col", 0)
 
 
 def gather_over_rows(values):

time: 678 us -> 688 us (1.015)
  waiting for transfers between devices: 416 us -> 457 us
  blocking collectives: 125 us -> 89 us
    all_gather x4 -> x0, blocking collectives: 36.6 us -> none  [gather_over_cols(): return lax.all_gather(values, 'col', axis=0, tiled=True)]
    ppermute x0 -> x4, waiting for transfers between devices: none -> 18.7 us  [do_entries(): side_arr = lax.ppermute(earlier, axis_name=mesh_ax, perm=u_next)]
    reduce_scatter x4, waiting for transfers between devices: 24.5 us -> 40.6 us  [sum_over_cols(): lax.psum_scatter(partial_value, 'col', scatter_dimension=0, tiled=True)]
    unnamed x85 -> x94, local copies, waits for them, and re-layouts: 18.3 us -> 22 us
  transfers between devices with their start and end apart: 14 -> 18, of which waited for: 10 -> 14; matrix products, arithmetic and copies ran while one was open for 10% -> 9% of each run, Pallas kernels for 0% -> 0%
where the time goes in v1:
time: 688 us; the launch traced here: 687 us
  waiting for transfers between devices  457 us (66%)
  blocking collectives  89 us (13%)
  local copies, waits for them, and re-layouts  46.3 us (7%)
  matrix products  43.4 us (6%)
  other arithmetic  28.1 us (4%)
  between operations  15.2 us (2%)
  starting transfers between devices  8.09 us (1%)
    psum x1, waiting for transfers between devices, on_device(): lax.psum((query_wgrad, key_wgrad, value_wgrad, out_wgrad, col_gains[0], c...  304 us
    reduce_scatter x4, waiting for transfers between devices, sum_over_cols(): lax.psum_scatter(partial_value, 'col', scatter_dimension=0, tiled=True)  40.6 us
    reduce_scatter x4, waiting for transfers between devices, sum_over_rows(): lax.psum_scatter(partial_value, 'row', scatter_dimension=0, tiled=True)  37.8 us
    reduce_scatter x1, waiting for transfers between devices, on_device(): lax.psum_scatter(key_gradient.reshape(sequence_length, KEY_VALUE_HEADS *...  23.4 us
    psum x1, blocking collectives, on_device(): lax.psum((query_wgrad, key_wgrad, value_wgrad, out_wgrad, col_gains[0], c...  22.7 us
    unnamed x94, local copies, waits for them, and re-layouts  22 us
    dot_general x8, matrix products, matmul(): return jnp.dot(left, right, preferred_element_type=jnp.float32)  21 us
    ppermute x4, waiting for transfers between devices, do_entries(): side_arr = lax.ppermute(earlier, axis_name=mesh_ax, perm=u_next)  18.7 us
  transfers between devices with their start and end apart: 18, of which 14 were waited for; matrix products, arithmetic and copies ran while one was open for 9% of the time, Pallas kernels for 0%

profile of v1, /device:TPU:0, one launch (start us, length us, event | category | flops | bytes accessed | tf_op | source)
XLA Modules:
  0.0 686.7 jit_solution(6607611796754963276)
XLA Ops:
  8.4 2.6 psum.84
  12.1 2.9 collective-permute-start
  17.2 4.1 collective-permute-done
  22.6 2.1 fusion.18
  25.7 9.7 %reduce-scatter.11.cloned.1.call-done = f32[256,800]{0,1:T(8,128)} async-done(((f32[512,800]{0,1:T(8,128)}), f32[256,800]{0,1:T(8,128)}) %reduce-scatter.11.cloned.1.call-update) | async-done | bytes 819216 | tf_op jit(solution)/shard_map/reduce_scatter | solution.py:87
  35.4 1.9 copy_bitcast_fusion.1
  37.4 3.5 all-to-all-start
  41.1 7.3 %all-to-all-done = bf16[2,128,800]{1,2,0:T(8,128)(2,1)S(1)} async-done(((bf16[2,128,800]{1,2,0:T(8,128)(2,1)}), bf16[2,128,800]{1,2,0:T(8,128)(2,1)S(1)}, u32[]{:S(2)}, u32[]{:S(2)}) %all-to-all-start) | async-done | bytes 409632 | tf_op jit(solution)/shard_map/all_to_all | solution.py:95
  48.4 10.6 %all_gather.20 = bf16[512,320]{0,1:T(8,128)(2,1)S(1)} all-gather(bf16[128,320]{0,1:T(8,128)(2,1)S(1)} %bitcast.181), channel_id=1, replica_groups=mesh['dp'=8,'row'=2,'col'=2] {'row','col'}, dimensions={0}, use_global_device_ids=true | all-gather | bytes 409600 | tf_op jit(solution)/shard_map/all_gather | solution.py:181
  59.0 10.6 %all_gather.21 = bf16[512,320]{0,1:T(8,128)(2,1)S(1)} all-gather(bf16[128,320]{0,1:T(8,128)(2,1)S(1)} %bitcast.182), channel_id=1, replica_groups=mesh['dp'=8,'row'=2,'col'=2] {'row','col'}, dimensions={0}, use_global_device_ids=true | all-gather | bytes 409600 | tf_op jit(solution)/shard_map/all_gather | solution.py:175
  73.6 8.1 %all_to_all.67 = bf16[128,2,480]{0,2,1:T(8,128)(2,1)S(1)} all-to-all(bf16[128,2,480]{0,2,1:T(8,128)(2,1)S(1)} %bitcast.169), channel_id=1, replica_groups=mesh['dp'=8,'row'=2,'col'=2] {'col'}, dimensions={1} | all-to-all | bytes 491520 | tf_op jit(solution)/shard_map/all_to_all | solution.py:99
  81.7 2.2 all_gather.22
  85.7 19.6 %reduce-scatter.13.cloned.1.call-done = f32[256,480]{0,1:T(8,128)} async-done(((f32[512,480]{0,1:T(8,128)}), f32[256,480]{0,1:T(8,128)}) %reduce-scatter.13.cloned.1.call-update) | async-done | bytes 491536 | tf_op jit(solution)/shard_map/reduce_scatter | solution.py:91
  106.4 2.5 psum.85
  110.2 7.0 %collective-permute-done.1 = bf16[1,256,480]{1,2,0:T(8,128)(2,1)S(1)} collective-permute-done((bf16[1,256,480]{1,2,0:T(8,128)(2,1)S(1)}, bf16[1,256,480]{1,2,0:T(8,128)(2,1)S(1)}, u32[]{:S(2)}, u32[]{:S(2)}) %collective-permute-start.1) | collective-permute-done | bytes 245792 | tf_op jit(solution)/shard_map/ppermute | solution.py:28
  119.1 2.3 fusion.40
  124.7 4.2 fusion.38
  129.0 3.2 reduce-scatter.19.cloned.1.call-done
  132.2 16.5 %reduce-scatter.15.cloned.1.call-done = f32[256,2560]{1,0:T(8,128)} async-done(((f32[512,2560]{1,0:T(8,128)}), f32[256,2560]{1,0:T(8,128)}) %reduce-scatter.15.cloned.1.call-update) | async-done | bytes 2621456 | tf_op jit(solution)/shard_map/reduce_scatter | solution.py:87
  148.7 3.7 multiply_convert_fusion.1
  153.6 12.7 %all-gather.5.cloned.1.call-done = bf16[512,2560]{1,0:T(8,128)(2,1)} async-done(((bf16[256,2560]{1,0:T(8,128)(2,1)}), bf16[512,2560]{1,0:T(8,128)(2,1)}) %all-gather.5.cloned.1.call-update) | async-done | bytes 2621456 | tf_op jit(solution)/shard_map/all_gather | solution.py:83
  166.4 4.9 fusion.41
  171.3 20.9 %reduce-scatter.21.cloned.1.call-done = f32[256,480]{0,1:T(8,128)} async-done(((f32[512,480]{0,1:T(8,128)}), f32[256,480]{0,1:T(8,128)}) %reduce-scatter.21.cloned.1.call-update) | async-done | bytes 491536 | tf_op jit(solution)/shard_map/reduce_scatter | solution.py:91
  192.3 1.9 multiply_reduce_fusion
  194.1 2.6 psum.86
  198.4 7.7 %collective-permute-done.3 = bf16[1,256,480]{1,2,0:T(8,128)(2,1)S(1)} collective-permute-done((bf16[1,256,480]{1,2,0:T(8,128)(2,1)S(1)}, bf16[1,256,480]{1,2,0:T(8,128)(2,1)S(1)}, u32[]{:S(2)}, u32[]{:S(2)}) %collective-permute-start.3) | collective-permute-done | bytes 245792 | tf_op jit(solution)/shard_map/ppermute | solution.py:28
  207.7 8.4 %reduce-scatter.23.cloned.1.call-done = f32[256,480]{0,1:T(8,128)} async-done(((f32[512,480]{0,1:T(8,128)}), f32[256,480]{0,1:T(8,128)}) %reduce-scatter.23.cloned.1.call-update) | async-done | bytes 491536 | tf_op jit(solution)/shard_map/reduce_scatter | solution.py:87
  217.2 8.2 %all_to_all.68 = bf16[2,128,480]{1,2,0:T(8,128)(2,1)S(1)} all-to-all(bf16[2,128,480]{1,2,0:T(8,128)(2,1)S(1)} %copy_bitcast_fusion.3), channel_id=1, replica_groups=mesh['dp'=8,'row'=2,'col'=2] {'col'}, dimensions={0} | all-to-all | bytes 491520 | tf_op jit(solution)/shard_map/all_to_all | solution.py:95
  225.5 4.1 fusion.24
  230.8 3.8 fusion.2
  238.2 2.1 fusion.42
  241.1 11.2 %reduce-scatter.27.cloned.1.call-done = f32[128,320]{0,1:T(8,128)} async-done(((f32[512,320]{0,1:T(8,128)}), f32[128,320]{0,1:T(8,128)}) %reduce-scatter.27.cloned.1.call-update) | async-done | bytes 163856 | tf_op jit(solution)/shard_map/reduce_scatter | solution.py:277
  253.8 23.4 %reduce-scatter.25.cloned.1.call-done = f32[128,320]{0,1:T(8,128)} async-done(((f32[512,320]{0,1:T(8,128)}), f32[128,320]{0,1:T(8,128)}) %reduce-scatter.25.cloned.1.call-update) | async-done | bytes 163856 | tf_op jit(solution)/shard_map/reduce_scatter | solution.py:271
  279.4 9.2 %all_to_all.69 = bf16[128,2,800]{0,2,1:T(8,128)(2,1)S(1)} all-to-all(bf16[128,2,800]{0,2,1:T(8,128)(2,1)S(1)} %pad_maximum_fusion.2), channel_id=1, replica_groups=mesh['dp'=8,'row'=2,'col'=2] {'col'}, dimensions={1} | all-to-all | bytes 819200 | tf_op jit(solution)/shard_map/all_to_all | solution.py:99
  288.6 2.4 all_gather.25
  293.6 3.7 convolution_bitcast_fusion
  297.3 6.5 copy.90
  303.8 3.1 fusion.39
  307.0 3.2 fusion.45
  310.2 2.5 slice_bitcast_fusion
  312.7 6.4 copy.88
  319.1 6.6 copy.89
  332.8 4.9 all-reduce.5
  337.8 22.7 %all-reduce.3 = (f32[480]{0:T(512)}, f32[480]{0:T(512)}) all-reduce(f32[480]{0:T(512)S(1)} %get-tuple-element.68, f32[480]{0:T(512)S(1)} %get-tuple-element.69), channel_id=1, replica_groups=mesh['dp'=8,'row'=2,'col'=2] {'dp'}, use_global_device_ids=true, to_apply=%region_23.24 | all-reduce | flops 960 | bytes 7680 | tf_op jit(solution)/shard_map/psum | solution.py:312
  360.4 2.4 psum.87
  362.9 2.3 fusion.14
  365.2 304.2 %all-reduce.8.cloned.1.call-done = (f32[480,480]{0,1:T(8,128)}, f32[480,160]{0,1:T(8,128)}, f32[480,160]{0,1:T(8,128)}, f32[480,480]{1,0:T(8,128)}, f32[1,480,12...) async-done(((f32[480,480]{0,1:T(8,128)}, f32[480,160]{0,1:T(8,128)}, f32[480,160]{0,1:T(8,128)}, f32[480,480]{1,0:T(8,128)}, ...) | async-done | bytes 9830416 | tf_op jit(solution)/shard_map/psum | solution.py:312
  669.4 2.5 copy.91
  (184 shorter events, 52.5 us)
Async XLA Ops:
  7.2 112.0 %copy-start = (bf16[1280,480]{0,1:T(8,128)(2,1)S(1)}, bf16[1280,480]{0,1:T(8,128)(2,1)}, u32[]{:S(2)}) copy-start(bf16[1280,480]{0,1:T(8,128)(2,1)} %param.24) | copy-start | bytes 3686404
  7.2 15.3 %copy-start.37 = (bf16[480,480]{1,0:T(8,128)(2,1)S(1)}, bf16[480,480]{1,0:T(8,128)(2,1)}, u32[]{:S(2)}) copy-start(bf16[480,480]{1,0:T(8,128)(2,1)} %param.17) | copy-start | bytes 1382404
  7.2 28.2 %reduce-scatter.11.cloned.1.call-start = ((), (), s32[]{:S(2)}) async-start(), calls=%async_computation.14 | async-start | bytes 2457600 | tf_op jit(solution)/shard_map/reduce_scatter | solution.py:87
  12.1 9.2 %collective-permute-start = (bf16[1,256,480]{1,2,0:T(8,128)(2,1)S(1)}, bf16[1,256,480]{1,2,0:T(8,128)(2,1)S(1)}, u32[]{:S(2)}, u32[]{:S(2)}) collective-permute-start(bf16[1,256,480]{1,2,0:T(8,128)(2,1)S(1)} %fusion.21), channel_id=1, source_target_pairs={{0,1},{1,0},{2,3},{3,2},{4,5},{5,4},{6,7},{7,6},{8,9},{9,8},{10,11... | collective-permute-start | bytes 737288 | tf_op jit(solution)/shard_map/ppermute | solution.py:28
  16.1 8.6 %copy-start.27 = (bf16[480,160]{1,0:T(8,128)(2,1)}, bf16[480,160]{1,0:T(8,128)(2,1)S(1)}, u32[]{:S(2)}) copy-start(bf16[480,160]{1,0:T(8,128)(2,1)S(1)} %copy.76) | copy-start | bytes 460804
  17.2 7.5 %copy-start.29 = (bf16[480,160]{1,0:T(8,128)(2,1)}, bf16[480,160]{1,0:T(8,128)(2,1)S(1)}, u32[]{:S(2)}) copy-start(bf16[480,160]{1,0:T(8,128)(2,1)S(1)} %copy.75) | copy-start | bytes 460804
  22.5 2.2 copy-start.12
  22.5 2.2 copy-start.36
  37.4 11.0 %all-to-all-start = ((bf16[2,128,800]{1,2,0:T(8,128)(2,1)}), bf16[2,128,800]{1,2,0:T(8,128)(2,1)S(1)}, u32[]{:S(2)}, u32[]{:S(2)}) async-start(bf16[2,128,800]{1,2,0:T(8,128)(2,1)} %copy_bitcast_fusion.1), calls=%async_computation.1 | async-start | bytes 819200 | tf_op jit(solution)/shard_map/all_to_all | solution.py:95
  40.9 64.4 %reduce-scatter.13.cloned.1.call-start = ((), (), s32[]{:S(2)}) async-start(), calls=%async_computation.15 | async-start | bytes 1474560 | tf_op jit(solution)/shard_map/reduce_scatter | solution.py:91
  59.0 12.5 %copy-start.24 = (bf16[512,320]{0,1:T(8,128)(2,1)}, bf16[512,320]{0,1:T(8,128)(2,1)S(1)}, u32[]{:S(2)}) copy-start(bf16[512,320]{0,1:T(8,128)(2,1)S(1)} %all_gather.20) | copy-start | bytes 983044
  69.7 1.6 copy-start.17
  70.5 3.0 copy-start.1
  72.5 11.3 %copy-start.14 = (bf16[480,480]{1,0:T(8,128)(2,1)S(1)}, bf16[480,480]{1,0:T(8,128)(2,1)}, u32[]{:S(2)}) copy-start(bf16[480,480]{1,0:T(8,128)(2,1)} %param.20) | copy-start | bytes 1382404
  73.5 8.1 %copy-start.22 = (bf16[5,64,3,128]{3,1,2,0:T(8,128)(2,1)}, bf16[5,64,3,128]{3,1,2,0:T(8,128)(2,1)S(1)}, u32[]{:S(2)}) copy-start(bf16[5,64,3,128]{3,1,2,0:T(8,128)(2,1)S(1)} %convolution_convert_fusion) | copy-start | bytes 737284
  73.6 11.8 %copy-start.10 = (bf16[256,480]{0,1:T(8,128)(2,1)S(1)}, bf16[256,480]{0,1:T(8,128)(2,1)}, u32[]{:S(2)}) copy-start(bf16[256,480]{0,1:T(8,128)(2,1)} %param.25) | copy-start | bytes 737284
  73.6 31.7 %copy-start.2 = (bf16[256,480]{0,1:T(8,128)(2,1)S(1)}, bf16[256,480]{0,1:T(8,128)(2,1)}, u32[]{:S(2)}) copy-start(bf16[256,480]{0,1:T(8,128)(2,1)} %param.13) | copy-start | bytes 737284
  81.7 27.3 %copy-start.32 = (f32[480]{0:T(512)S(1)}, f32[480]{0:T(512)}, u32[]{:S(2)}) copy-start(f32[480]{0:T(512)} %param.21) | copy-start | bytes 5764
  85.3 46.9 %reduce-scatter.19.cloned.1.call-start = ((), (), s32[]{:S(2)}) async-start(), calls=%async_computation.19 | async-start | bytes 3932160 | tf_op jit(solution)/shard_map/reduce_scatter | solution.py:87
  85.3 24.2 %collective-permute-start.2 = (bf16[1,256,480]{1,2,0:T(8,128)(2,1)S(1)}, bf16[1,256,480]{1,2,0:T(8,128)(2,1)S(1)}, u32[]{:S(2)}, u32[]{:S(2)}) collective-permute-start(bf16[1,256,480]{1,2,0:T(8,128)(2,1)S(1)} %bitcast.159), channel_id=1, source_target_pairs={{0,1},{1,0},{2,3},{3,2},{4,5},{5,4},{6,7},{7,6},{8,9},{9,8},{10,11... | collective-permute-start | bytes 737288 | tf_op jit(solution)/shard_map/ppermute | solution.py:28
  109.1 8.1 %collective-permute-start.1 = (bf16[1,256,480]{1,2,0:T(8,128)(2,1)S(1)}, bf16[1,256,480]{1,2,0:T(8,128)(2,1)S(1)}, u32[]{:S(2)}, u32[]{:S(2)}) collective-permute-start(bf16[1,256,480]{1,2,0:T(8,128)(2,1)S(1)} %fusion.20), channel_id=1, source_target_pairs={{0,1},{1,0},{2,3},{3,2},{4,5},{5,4},{6,7},{7,6},{8,9},{9,8},{10,11... | collective-permute-start | bytes 737288 | tf_op jit(solution)/shard_map/ppermute | solution.py:28
  121.5 27.2 %reduce-scatter.15.cloned.1.call-start = ((), (), s32[]{:S(2)}) async-start(), calls=%async_computation.16 | async-start | bytes 7864320 | tf_op jit(solution)/shard_map/reduce_scatter | solution.py:87
  121.6 1.7 copy-start.16
  129.0 37.4 %all-gather.5.cloned.1.call-start = ((), (), s32[]{:S(2)}) async-start(), calls=%async_computation.20 | async-start | bytes 3932160 | tf_op jit(solution)/shard_map/all_gather | solution.py:83
  153.6 38.7 %reduce-scatter.21.cloned.1.call-start = ((), (), s32[]{:S(2)}) async-start(), calls=%async_computation.21 | async-start | bytes 1474560 | tf_op jit(solution)/shard_map/reduce_scatter | solution.py:91
  171.3 44.9 %reduce-scatter.23.cloned.1.call-start = ((), (), s32[]{:S(2)}) async-start(), calls=%async_computation.22 | async-start | bytes 1474560 | tf_op jit(solution)/shard_map/reduce_scatter | solution.py:87
  196.7 9.5 %copy-start.15 = (bf16[480,480]{1,0:T(8,128)(2,1)S(1)}, bf16[480,480]{1,0:T(8,128)(2,1)}, u32[]{:S(2)}) copy-start(bf16[480,480]{1,0:T(8,128)(2,1)} %param.20) | copy-start | bytes 1382404
  198.0 8.1 %collective-permute-start.3 = (bf16[1,256,480]{1,2,0:T(8,128)(2,1)S(1)}, bf16[1,256,480]{1,2,0:T(8,128)(2,1)S(1)}, u32[]{:S(2)}, u32[]{:S(2)}) collective-permute-start(bf16[1,256,480]{1,2,0:T(8,128)(2,1)S(1)} %convert_bitcast_fusion.2), channel_id=1, source_target_pairs={{0,1},{1,0},{2,3},{3,2},{4,5},{5,4},{6,7},{7,6},{8,9},{9,8},{10,11... | collective-permute-start | bytes 737288 | tf_op jit(solution)/shard_map/ppermute | solution.py:28
  207.7 44.6 %reduce-scatter.27.cloned.1.call-start = ((), (), s32[]{:S(2)}) async-start(), calls=%async_computation.24 | async-start | bytes 819200 | tf_op jit(solution)/shard_map/reduce_scatter | solution.py:277
  225.5 4.1 copy-start.23
  229.6 47.7 %reduce-scatter.25.cloned.1.call-start = ((), (), s32[]{:S(2)}) async-start(), calls=%async_computation.23 | async-start | bytes 819200 | tf_op jit(solution)/shard_map/reduce_scatter | solution.py:271
  230.8 5.1 copy-start.18
  230.8 5.1 copy-start.20
  237.5 56.1 %all-gather.3.cloned.1.call-start = ((), (), s32[]{:S(2)}) async-start(), calls=%async_computation.17 | async-start | bytes 1966080 | tf_op jit(solution)/shard_map/all_gather | solution.py:83
  238.1 93.4 %reduce-scatter.29.cloned.1.call-start = ((), (), s32[]{:S(2)}) async-start(), calls=%async_computation.25 | async-start | bytes 1474560 | tf_op jit(solution)/shard_map/reduce_scatter | solution.py:91
  277.3 14.6 %copy-start.28 = (bf16[480,160]{1,0:T(8,128)(2,1)S(1)}, bf16[480,160]{1,0:T(8,128)(2,1)}, u32[]{:S(2)}) copy-start(bf16[480,160]{1,0:T(8,128)(2,1)} %copy-done.27) | copy-start | bytes 460804
  277.3 14.6 %copy-start.30 = (bf16[480,160]{1,0:T(8,128)(2,1)S(1)}, bf16[480,160]{1,0:T(8,128)(2,1)}, u32[]{:S(2)}) copy-start(bf16[480,160]{1,0:T(8,128)(2,1)} %copy-done.29) | copy-start | bytes 460804
  277.3 14.6 %copy-start.38 = (bf16[480,480]{1,0:T(8,128)(2,1)S(1)}, bf16[480,480]{1,0:T(8,128)(2,1)}, u32[]{:S(2)}) copy-start(bf16[480,480]{1,0:T(8,128)(2,1)} %param.17) | copy-start | bytes 1382404
  293.5 69.3 %reduce-scatter.17.cloned.1.call-start = ((), (), s32[]{:S(2)}) async-start(), calls=%async_computation.18 | async-start | bytes 1474560 | tf_op jit(solution)/shard_map/reduce_scatter | solution.py:91
  306.9 362.5 %all-reduce.8.cloned.1.call-start = ((), (), s32[]{:S(2)}) async-start(), calls=%async_computation.26 | async-start | bytes 20971520 | tf_op jit(solution)/shard_map/psum | solution.py:312
  319.1 8.0 %copy-start.13 = (bf16[2,60,8,256]{3,2,0,1:T(8,128)(2,1)S(1)}, bf16[2,60,8,256]{3,2,0,1:T(8,128)(2,1)}, u32[]{:S(2)}) copy-start(bf16[2,60,8,256]{3,2,0,1:T(8,128)(2,1)} %copy-done.12) | copy-start | bytes 1474564
  329.6 1.9 copy-start.33
  329.6 3.2 copy-start.35
  329.6 33.3 %copy-start.5 = (f32[256,480]{0,1:T(8,128)S(1)}, f32[256,480]{0,1:T(8,128)}, u32[]{:S(2)}) copy-start(f32[256,480]{0,1:T(8,128)} %reduce-scatter.21.cloned.1.call-done) | copy-start | bytes 1474564
  329.7 33.2 %copy-start.11 = (bf16[256,480]{0,1:T(8,128)(2,1)S(1)}, bf16[256,480]{0,1:T(8,128)(2,1)}, u32[]{:S(2)}) copy-start(bf16[256,480]{0,1:T(8,128)(2,1)} %param.25) | copy-start | bytes 737284
  671.9 5.9 copy-start.26
  671.9 6.7 copy-start.25
  673.2 6.1 copy-start.21
  (10 other events, 10.8 us)
Sparse Core Ops, SparseCore 0:
  24.8 10.5 reduce-scatter.10
  85.4 19.8 reduce-scatter.12
  121.6 10.4 reduce-scatter.18
  134.3 14.3 reduce-scatter.14
  153.7 12.6 all-gather.4
  171.4 20.8 reduce-scatter.20
  207.8 8.3 reduce-scatter.22
  229.7 22.5 reduce-scatter.26
  254.8 22.4 reduce-scatter.24
  279.2 9.3 all-gather.2
  293.7 19.6 reduce-scatter.28
  316.1 19.6 reduce-scatter.16
  341.9 327.5 all-reduce.7
